TPU v7x, 32 devices: a whole 2x2x4 slice. The times are simulated.
32 devices in a mesh: dp: 16 (over z, y, x), mp: 2 (over core).
Axes of the slice: x: 2, y: 2, z: 4, core: 2. Of those that a mesh axis runs over, the one named last changes fastest.
Arguments:
- inputs: bfloat16 [6144, 768], P('dp')
- cotangent: bfloat16 [6144, 768], P('dp'), may hold values from -6 to 6
- lengths: int32 [16, 3], P('dp'), may hold values from 0 to 192, as said below
- masked: int32 [6144], P('dp'), may hold values 0 or 1
- replace_ids: int32 [6144], P('dp'), may hold values from 0 to 15359, as said below
- attention_master: float32 [4, 768, 768], P(None, 'dp', 'mp')
- attention_moment: float32 [4, 768, 768], P(None, 'dp', 'mp'), may hold values from -0.1875 to 0.1875
- attention_square: float32 [4, 768, 768], P(None, 'dp', 'mp'), may hold values from 0.00016276042 to 0.0006510417
- geglu_master: float32 [3, 768, 3072], P(None, 'dp', 'mp')
- geglu_moment: float32 [3, 768, 3072], P(None, 'dp', 'mp'), may hold values from -0.1875 to 0.1875
- geglu_square: float32 [3, 768, 3072], P(None, 'dp', 'mp'), may hold values from 0.00016276042 to 0.0006510417
- embed_master: float32 [15360, 768], P('dp', 'mp'), may hold values from -6 to 6
- embed_moment: float32 [15360, 768], P('dp', 'mp'), may hold values from -0.0008544922 to 0.0008544922
- embed_square: float32 [15360, 768], P('dp', 'mp'), may hold values from 3.1789145e-09 to 1.2715658e-08
- norms_master: float32 [4, 768], replicated
- norms_moment: float32 [4, 768], replicated, may hold values from -0.1875 to 0.1875
- norms_square: float32 [4, 768], replicated, may hold values from 0.00016276042 to 0.0006510417
Outputs:
- output: float32 [6144, 768], P('dp')
- input_grad: float32 [6144, 768], P('dp')
- rms_stats: float32 [3], replicated
- lamb_norms: float32 [2, 12], replicated
- attention_grad: float32 [4, 768, 768], P(None, 'dp', 'mp')
- attention_first: float32 [4, 768, 768], P(None, 'dp', 'mp')
- attention_second: float32 [4, 768, 768], P(None, 'dp', 'mp')
- attention_new: float32 [4, 768, 768], P(None, 'dp', 'mp')
- geglu_grad: float32 [3, 768, 3072], P(None, 'dp', 'mp')
- geglu_first: float32 [3, 768, 3072], P(None, 'dp', 'mp')
- geglu_second: float32 [3, 768, 3072], P(None, 'dp', 'mp')
- geglu_new: float32 [3, 768, 3072], P(None, 'dp', 'mp')
- embed_grad: float32 [15360, 768], P('dp', 'mp')
- embed_first: float32 [15360, 768], P('dp', 'mp')
- embed_second: float32 [15360, 768], P('dp', 'mp')
- embed_new: float32 [15360, 768], P('dp', 'mp')
- norms_grad: float32 [4, 768], replicated
- norms_first: float32 [4, 768], replicated
- norms_second: float32 [4, 768], replicated
- norms_new: float32 [4, 768], replicated
Inputs may be any that keep to these rules, and one draw needn't show every extreme that they name: Row d lists the lengths of the sequences given to device d, zeros after; each sequence has 128 tokens or more; a row sums to at most 384, and some row reaches it with a sequence of 192. `replace_ids`: among the 384 slots of one device, exactly 24 ids fall in each aligned block of 960 table rows.
All inputs are finite; a program needn't handle non-finite values. No bound on the sum of `masked` on one device may be relied on, other than what follows from the above.
Results may differ from a plain program's by a relative error of at most 0.016.
The roundings to bfloat16 on the way count: a program that leaves them out, or rounds other values in their place, can miss the bound.
Values may be sent and summed in bfloat16 or wider, within the bound.
A program may use at most 192 MiB of HBM per device.

v0:
```python
import math
import jax
import jax.numpy as jnp
from jax import lax
from jax.sharding import PartitionSpec as P

HEADS = 12
STEP_COUNT = 6
first_decay = 0.5
second_decay = 0.5
learn_rate = 0.3
matrix_decay = 0.01
adam_epsilon = 1e-06
norm_epsilon = 1e-12
masked_score = -1000000000.0


def cut_along(value, dim, length):
    dims = value.shape
    tiles = value.reshape(*dims[:dim], length, dims[dim] // length, *dims[dim + 1 :])
    return jnp.moveaxis(tiles, dim, 0)


def sent_and_summed(value, axis, dim):
    length = lax.axis_size(axis)
    tiles = lax.all_to_all(cut_along(value, dim, length), axis, 0, 0, tiled=True)
    return jnp.sum(tiles.astype(jnp.float32), axis=0)


def layer_norm(values, gain_row, shift_row):
    center = values - jnp.mean(values, axis=-1, keepdims=True)
    spread = jnp.mean(center * center, axis=-1, keepdims=True)
    return center * lax.rsqrt(spread + norm_epsilon) * gain_row + shift_row


def norm_pair(values, gain_pair):
    return layer_norm(values, gain_pair[0], gain_pair[1])


def lamb_parts(master, moment, square, gradient, decay_rate):
    new_moment = first_decay * moment + (1.0 - first_decay) * gradient
    new_square = second_decay * square + (1.0 - second_decay) * gradient * gradient
    update = (
        new_moment
        / (1.0 - first_decay**STEP_COUNT)
        / (jnp.sqrt(new_square / (1.0 - second_decay**STEP_COUNT)) + adam_epsilon)
        + decay_rate * master
    )
    return (new_moment, new_square, update)


def gelu_tanh(values):
    return jax.nn.gelu(values, approximate=True)


def local(
    inputs,
    cotangent,
    lengths,
    masked,
    replace_ids,
    attention_master,
    attention_moment,
    attention_square,
    geglu_master,
    geglu_moment,
    geglu_square,
    embed_master,
    embed_moment,
    embed_square,
    norms_master,
    norms_moment,
    norms_square,
):
    half_type = jnp.bfloat16
    full_type = jnp.float32
    tokens_here = inputs.shape[0]
    width = inputs.shape[1]
    head_dim = width // HEADS
    local_heads = HEADS // lax.axis_size("mp")
    block_len = min(tokens_here, 512)
    attn_scale = 1.0 / math.sqrt(head_dim)
    column_count = embed_master.shape[1]
    attn_low, geglu_low = (
        lax.all_gather(attention_master.astype(half_type), "dp", axis=1, tiled=True),
        lax.all_gather(geglu_master.astype(half_type), "dp", axis=1, tiled=True),
    )
    owners = lax.axis_size("dp")
    owner_rows = embed_master.shape[0]
    per_owner = tokens_here // owners
    owner_low = jnp.arange(owners, dtype=jnp.int32)[:, None] * owner_rows
    owned = (replace_ids[None, :] >= owner_low) & (replace_ids[None, :] < owner_low + owner_rows)
    order = jnp.arange(tokens_here, dtype=jnp.int32)
    earlier = (order[:, None] < order[None, :]).astype(half_type)
    rank = jnp.dot(owned.astype(half_type), earlier, preferred_element_type=full_type)
    owner_at = jnp.arange(owners, dtype=full_type)[:, None] * per_owner
    target = jnp.sum(jnp.where(owned, rank + owner_at, 0.0), axis=0).astype(jnp.int32)
    moves = target[None, :] == order[:, None]
    sorted_ids = jnp.sum(jnp.where(moves, replace_ids[None, :], 0), axis=1)
    asked = lax.all_to_all(sorted_ids, "dp", 0, 0, tiled=True)
    asked = asked - lax.axis_index("dp") * owner_rows
    hits = asked[:, None] == jnp.arange(owner_rows, dtype=jnp.int32)[None, :]
    sent_rows = jnp.dot(
        hits.astype(half_type), embed_master.astype(half_type), preferred_element_type=full_type
    ).astype(half_type)
    got_rows = lax.all_to_all(sent_rows, "dp", 0, 0, tiled=True)
    looked_cols = jnp.einsum(
        "pt,pc->tc", moves.astype(half_type), got_rows, preferred_element_type=full_type
    ).astype(half_type)
    looked = lax.all_gather(looked_cols, "mp", axis=1, tiled=True)
    is_masked = masked[:, None] == 1
    hidden_in = jnp.where(is_masked, looked.astype(full_type), inputs.astype(full_type))
    length_row = lengths[0]
    places = jnp.arange(tokens_here, dtype=jnp.int32)
    ends_at = jnp.cumsum(length_row)
    segment_ids = jnp.sum((ends_at[None, :] <= places[:, None]).astype(jnp.int32), axis=1)
    live_rows = (places < jnp.sum(length_row)).astype(full_type)[:, None]
    token_count = jnp.sum(length_row).astype(full_type)
    head_ids = lax.axis_index("mp") * local_heads + jnp.arange(local_heads, dtype=jnp.int32)
    slopes = 2.0 ** (-8.0 * (head_ids.astype(full_type) + 1.0) / HEADS)
    act_low = hidden_in.astype(half_type)
    qkv_low = jnp.einsum(
        "td,kdc->ktc", act_low, attn_low[:3], preferred_element_type=full_type
    ).astype(half_type)
    head_vals = qkv_low.reshape(3, tokens_here, local_heads, head_dim)

    def block_scores(begin_at, query_blk):
        query_pos = begin_at + jnp.arange(block_len, dtype=jnp.int32)
        scores = (
            jnp.einsum("qhe,khe->hqk", query_blk, head_vals[1], preferred_element_type=full_type)
            * attn_scale
        )
        distance = jnp.abs(query_pos[:, None] - places[None, :]).astype(full_type)
        scores = scores - slopes[:, None, None] * distance[None]
        same_seq = segment_ids[:, None] == segment_ids[None, :]
        return jnp.where(same_seq[None], scores, masked_score)

    def forward_block(begin_at):
        query_blk = head_vals[0]
        scores = block_scores(begin_at, query_blk)
        top_score = jnp.max(scores, axis=-1, keepdims=True)
        raised = jnp.exp(scores - top_score)
        row_total = jnp.sum(raised, axis=-1, keepdims=True)
        weights = (raised / row_total).astype(half_type)
        context_blk = jnp.einsum(
            "hqk,khe->qhe", weights, head_vals[2], preferred_element_type=full_type
        )
        return (context_blk.astype(half_type), (top_score + jnp.log(row_total))[..., 0])

    starts = jnp.arange(tokens_here // block_len, dtype=jnp.int32) * block_len
    context_blocks, lse_blocks = lax.map(forward_block, starts)
    context = context_blocks.reshape(tokens_here, local_heads * head_dim)
    attn_part = jnp.einsum("tc,dc->td", context, attn_low[3], preferred_element_type=full_type)
    attn_out = lax.psum(attn_part, "mp")
    normed_one, first_back = jax.vjp(norm_pair, hidden_in + attn_out, norms_master[0:2])
    normed_low = normed_one.astype(half_type)
    gate_up = jnp.einsum("td,kdf->ktf", normed_low, geglu_low[:2], preferred_element_type=full_type)
    gelu_val, gelu_back = jax.vjp(gelu_tanh, gate_up[0])
    inner_act = (gelu_val * gate_up[1]).astype(half_type)
    geglu_part = jnp.einsum("tf,df->td", inner_act, geglu_low[2], preferred_element_type=full_type)
    geglu_out = lax.psum(geglu_part, "mp")
    result, second_back = jax.vjp(norm_pair, normed_one + geglu_out, norms_master[2:4])
    squares = jnp.stack(
        [
            jnp.sum(hidden_in * hidden_in * live_rows),
            jnp.sum(attn_out * attn_out * live_rows),
            jnp.sum(geglu_out * geglu_out * live_rows),
        ]
    )
    count_total, square_total = lax.psum((token_count, squares), "dp")
    rms_stats = jnp.sqrt(square_total / (count_total * width) + 1e-06)
    grad_second, norm_grad_two = second_back(cotangent.astype(full_type) * live_rows)
    grad_geglu = grad_second.astype(half_type)
    grad_inner = jnp.einsum("td,df->tf", grad_geglu, geglu_low[2], preferred_element_type=full_type)
    down_grad = jnp.einsum("td,tf->df", grad_geglu, inner_act, preferred_element_type=full_type)
    grad_gate = gelu_back(grad_inner * gate_up[1])[0]
    grad_up = grad_inner * gelu_val
    grad_gu = jnp.stack([grad_gate, grad_up]).astype(half_type)
    gu_grad = jnp.einsum("td,ktf->kdf", normed_low, grad_gu, preferred_element_type=full_type)
    geglu_local = jnp.concatenate([gu_grad, down_grad[None]], axis=0)
    back_part = jnp.einsum("ktf,kdf->td", grad_gu, geglu_low[:2], preferred_element_type=full_type)
    grad_normed = grad_second + lax.psum(back_part, "mp")
    grad_first_in, norm_grad_one = first_back(grad_normed)
    grad_attn = grad_first_in.astype(half_type)
    grad_context = jnp.einsum(
        "td,dc->tc", grad_attn, attn_low[3], preferred_element_type=full_type
    ).astype(half_type)
    out_grad = jnp.einsum("td,tc->dc", grad_attn, context, preferred_element_type=full_type)
    grad_heads = grad_context.reshape(tokens_here, local_heads, head_dim)

    def backward_block(carry, packed):
        key_acc, value_acc = carry
        begin_at, lse_blk = packed
        query_blk = head_vals[0]
        scores = block_scores(begin_at, query_blk)
        weights = jnp.exp(scores - lse_blk[..., None])
        grad_weights = jnp.einsum(
            "qhe,khe->hqk", grad_heads, head_vals[2], preferred_element_type=full_type
        )
        value_acc = value_acc + jnp.einsum(
            "hqk,qhe->khe", weights.astype(half_type), grad_heads, preferred_element_type=full_type
        )
        row_inner = jnp.sum(grad_weights * weights, axis=-1, keepdims=True)
        grad_scores = (weights * (grad_weights - row_inner)).astype(half_type)
        grad_query = (
            jnp.einsum("hqk,khe->qhe", grad_scores, head_vals[1], preferred_element_type=full_type)
            * attn_scale
        )
        key_acc = (
            key_acc
            + jnp.einsum("hqk,qhe->khe", grad_scores, query_blk, preferred_element_type=full_type)
            * attn_scale
        )
        return ((key_acc, value_acc), grad_query.astype(half_type))

    zero_heads = jnp.zeros((tokens_here, local_heads, head_dim), full_type)
    (key_acc, value_acc), query_grads = lax.scan(
        backward_block, (zero_heads, zero_heads), (starts, lse_blocks)
    )
    grad_qkv = jnp.stack(
        [
            query_grads.reshape(tokens_here, -1),
            key_acc.reshape(tokens_here, -1).astype(half_type),
            value_acc.reshape(tokens_here, -1).astype(half_type),
        ]
    )
    qkv_grad = jnp.einsum("td,ktc->kdc", act_low, grad_qkv, preferred_element_type=full_type)
    act_part = jnp.einsum("ktc,kdc->td", grad_qkv, attn_low[:3], preferred_element_type=full_type)
    grad_in = grad_first_in + lax.psum(act_part.astype(jnp.bfloat16), "mp").astype(jnp.float32)
    input_grad = jnp.where(is_masked, 0.0, grad_in)
    attention_local = jnp.concatenate([qkv_grad, out_grad[None]], axis=0)
    own_columns = lax.dynamic_slice_in_dim(
        grad_in, lax.axis_index("mp") * column_count, column_count, 1
    )
    picked = jnp.where(is_masked, own_columns, 0.0)
    highest = lax.Precision.HIGHEST
    sorted_grads = jnp.dot(moves.astype(full_type), picked, precision=highest)
    got_grads = lax.all_to_all(sorted_grads, "dp", 0, 0, tiled=True)
    embed_summed = jnp.einsum("pr,pc->rc", hits.astype(full_type), got_grads, precision=highest)
    attention_summed, geglu_summed = (
        sent_and_summed(attention_local.astype(jnp.bfloat16), "dp", 1),
        sent_and_summed(geglu_local.astype(jnp.bfloat16), "dp", 1),
    )
    inverse_count = 1.0 / count_total
    attention_grad = attention_summed * inverse_count
    geglu_grad = geglu_summed * inverse_count
    embed_grad = embed_summed * inverse_count
    attention_first, attention_second, attention_update = lamb_parts(
        attention_master, attention_moment, attention_square, attention_grad, matrix_decay
    )
    geglu_first, geglu_second, geglu_update = lamb_parts(
        geglu_master, geglu_moment, geglu_square, geglu_grad, matrix_decay
    )
    embed_first, embed_second, embed_update = lamb_parts(
        embed_master, embed_moment, embed_square, embed_grad, matrix_decay
    )
    weight_squares = jnp.concatenate(
        [
            jnp.sum(attention_master * attention_master, axis=(1, 2)),
            jnp.sum(geglu_master * geglu_master, axis=(1, 2)),
            jnp.sum(embed_master * embed_master)[None],
        ]
    )
    update_squares = jnp.concatenate(
        [
            jnp.sum(attention_update * attention_update, axis=(1, 2)),
            jnp.sum(geglu_update * geglu_update, axis=(1, 2)),
            jnp.sum(embed_update * embed_update)[None],
        ]
    )
    norms_local = jnp.concatenate([norm_grad_one, norm_grad_two], axis=0)
    weight_total, update_total, norms_summed = lax.psum(
        (weight_squares, update_squares, norms_local * 0.5), ("dp", "mp")
    )
    weight_norms = jnp.sqrt(weight_total)
    update_norms = jnp.sqrt(update_total)
    ratios = weight_norms / update_norms
    attention_new = attention_master - learn_rate * ratios[0:4][:, None, None] * attention_update
    geglu_new = geglu_master - learn_rate * ratios[4:7][:, None, None] * geglu_update
    embed_new = embed_master - learn_rate * ratios[7] * embed_update
    norms_grad = norms_summed * inverse_count
    norms_first, norms_second, norms_update = lamb_parts(
        norms_master, norms_moment, norms_square, norms_grad, 0.0
    )
    norm_weight = jnp.sqrt(jnp.sum(norms_master * norms_master, axis=1))
    norm_update = jnp.sqrt(jnp.sum(norms_update * norms_update, axis=1))
    norms_new = norms_master - learn_rate * (norm_weight / norm_update)[:, None] * norms_update
    lamb_norms = jnp.stack(
        [jnp.concatenate([weight_norms, norm_weight]), jnp.concatenate([update_norms, norm_update])]
    )
    return (
        result,
        input_grad,
        rms_stats,
        lamb_norms,
        attention_grad,
        attention_first,
        attention_second,
        attention_new,
        geglu_grad,
        geglu_first,
        geglu_second,
        geglu_new,
        embed_grad,
        embed_first,
        embed_second,
        embed_new,
        norms_grad,
        norms_first,
        norms_second,
        norms_new,
    )


def solution(mesh):
    in_specs = (
        P("dp", None),
        P("dp", None),
        P("dp", None),
        P("dp"),
        P("dp"),
        P(None, "dp", "mp"),
        P(None, "dp", "mp"),
        P(None, "dp", "mp"),
        P(None, "dp", "mp"),
        P(None, "dp", "mp"),
        P(None, "dp", "mp"),
        P("dp", "mp"),
        P("dp", "mp"),
        P("dp", "mp"),
        P(),
        P(),
        P(),
    )
    out_specs = (
        P("dp", None),
        P("dp", None),
        P(),
        P(),
        P(None, "dp", "mp"),
        P(None, "dp", "mp"),
        P(None, "dp", "mp"),
        P(None, "dp", "mp"),
        P(None, "dp", "mp"),
        P(None, "dp", "mp"),
        P(None, "dp", "mp"),
        P(None, "dp", "mp"),
        P("dp", "mp"),
        P("dp", "mp"),
        P("dp", "mp"),
        P("dp", "mp"),
        P(),
        P(),
        P(),
        P(),
    )
    return jax.shard_map(local, mesh=mesh, in_specs=in_specs, out_specs=out_specs, check_vma=False)
```

profile of v0, /device:TPU:0, one launch (start us, length us, event | category | flops | bytes accessed | tf_op | source)
XLA Modules:
  0.0 669.8 jit_solution(15708946535372922440)
XLA Ops:
  7.2 1.8 copy.145
  11.7 8.3 %all-to-all-start = ((s32[16,24,1]{1,2,0:T(1,128)}), s32[16,24,1]{1,2,0:T(1,128)S(1)}, u32[]{:S(2)}, u32[]{:S(2)}) async-start(s32[16,24,1]{1,2,0:T(1,128)} %bitcast), calls=%async_computation | async-start | bytes 16384 | tf_op jit(solution)/shard_map/all_to_all | solution.py:100
  21.8 5.4 all-to-all-done
  28.7 3.5 all-to-all-start.1
  33.1 8.8 %all-to-all-done.1 = bf16[16,24,384]{2,1,0:T(8,128)(2,1)S(1)} async-done(((bf16[16,24,384]{2,1,0:T(8,128)(2,1)}), bf16[16,24,384]{2,1,0:T(8,128)(2,1)S(1)}, u32[]{:S(2)}, u32[]{:S(2)}) %all-to-all-start.1) | async-done | bytes 294944 | tf_op jit(solution)/shard_map/all_to_all | solution.py:106
  42.4 2.2 all_gather.9
  44.6 32.8 %all-gather.3.cloned.1.call-done = bf16[4,768,384]{2,0,1:T(4,128)(2,1)} async-done(((bf16[4,48,384]{2,0,1:T(4,128)(2,1)}), bf16[4,768,384]{2,0,1:T(4,128)(2,1)}) %all-gather.3.cloned.1.call-update) | async-done | bytes 2359312 | tf_op jit(solution)/shard_map/all_gather | solution.py:85
  77.4 4.1 copy.139
  90.5 1.5 fusion.79
  92.1 2.0 convert_element_type.187
  94.8 16.0 %all-reduce.11.cloned.1.call-done = f32[384,768]{1,0:T(8,128)} async-done(((f32[384,768]{1,0:T(8,128)}), f32[384,768]{1,0:T(8,128)}) %all-reduce.11.cloned.1.call-update) | async-done | bytes 1179664 | tf_op jit(solution)/shard_map/psum | solution.py:154
  110.8 2.0 fusion.110
  114.1 102.9 %all-gather.5.cloned.1.call-done = bf16[3,768,1536]{2,1,0:T(8,128)(2,1)} async-done(((bf16[3,48,1536]{2,1,0:T(8,128)(2,1)}), bf16[3,768,1536]{2,1,0:T(8,128)(2,1)}) %all-gather.5.cloned.1.call-update) | async-done | bytes 7077904 | tf_op jit(solution)/shard_map/all_gather | solution.py:86
  217.0 4.8 fusion.4
  225.0 3.8 fusion.31
  231.2 15.7 %all-reduce.13.cloned.1.call-done = f32[384,768]{1,0:T(8,128)} async-done(((f32[384,768]{1,0:T(8,128)}), f32[384,768]{1,0:T(8,128)}) %all-reduce.13.cloned.1.call-update) | async-done | bytes 1179664 | tf_op jit(solution)/shard_map/psum | solution.py:161
  247.0 2.2 fusion.108
  250.5 1.9 multiply_reduce_fusion.3
  252.4 1.7 fusion.107
  254.1 4.5 fusion.58
  260.0 3.0 fusion.40
  264.1 20.2 %all-reduce.15.cloned.1.call-done = f32[384,768]{1,0:T(8,128)} async-done(((f32[384,768]{1,0:T(8,128)}), f32[384,768]{1,0:T(8,128)}) %all-reduce.15.cloned.1.call-update) | async-done | bytes 1179664 | tf_op jit(solution)/shard_map/psum | solution.py:182
  284.3 4.1 multiply_reduce_fusion.4
  290.5 1.5 fusion.46
  297.1 2.8 fusion.44
  299.9 20.2 %all-reduce.17.cloned.1.call-done = bf16[384,768]{1,0:T(8,128)(2,1)} async-done(((bf16[384,768]{1,0:T(8,128)(2,1)}), bf16[384,768]{1,0:T(8,128)(2,1)}) %all-reduce.17.cloned.1.call-update) | async-done | bytes 589840 | tf_op jit(solution)/shard_map/psum | solution.py:229
  320.1 2.4 broadcast_select_fusion
  322.5 1.7 fusion.71
  324.2 6.8 %all-to-all-start.4 = ((f32[16,24,384]{2,1,0:T(8,128)}), f32[16,24,384]{2,1,0:T(8,128)}, u32[]{:S(2)}, u32[]{:S(2)}) async-start(f32[16,24,384]{2,1,0:T(8,128)} %bitcast.52), calls=%async_computation.4 | async-start | bytes 1179648 | tf_op jit(solution)/shard_map/all_to_all | solution.py:238
  331.1 2.5 convert_bitcast_fusion
  333.5 2.8 copy.121
  337.5 1.8 copy.124
  339.3 8.4 %all-to-all-done.4 = f32[16,24,384]{2,1,0:T(8,128)} async-done(((f32[16,24,384]{2,1,0:T(8,128)}), f32[16,24,384]{2,1,0:T(8,128)}, u32[]{:S(2)}, u32[]{:S(2)}) %all-to-all-start.4) | async-done | bytes 589856 | tf_op jit(solution)/shard_map/all_to_all | solution.py:238
  347.7 4.5 all-to-all-start.2
  352.3 6.6 convolution_convert_fusion
  360.3 2.6 fusion.8
  362.9 5.7 maximum_bitcast_fusion
  368.6 30.5 %all-to-all-done.2 = bf16[16,4,48,384]{3,2,1,0:T(8,128)(2,1)S(1)} async-done(((bf16[16,4,48,384]{3,2,1,0:T(8,128)(2,1)}), bf16[16,4,48,384]{3,2,1,0:T(8,128)(2,1)S(1)}, u32[]{:S(2)}, u32[]{:S(2)}) %all-to-all-start.2) | async-done | bytes 2359328 | tf_op jit(solution)/shard_map/all_to_all | solution.py:26
  399.1 10.9 %all-to-all-start.3 = ((bf16[16,3,48,1536]{3,2,1,0:T(8,128)(2,1)}), bf16[16,3,48,1536]{3,2,1,0:T(8,128)(2,1)}, u32[]{:S(2)}, u32[]{:S(2)}) async-start(bf16[16,3,48,1536]{3,2,1,0:T(8,128)(2,1)} %maximum_bitcast_fusion), calls=%async_computation.3 | async-start | bytes 14155776 | tf_op jit(solution)/shard_map/all_to_all | solution.py:26
  410.6 1.9 pad_maximum_fusion.9
  412.5 166.0 %all-reduce.5 = (f32[3]{0:T(128)S(1)}, f32[]{:T(128)}) all-reduce(f32[3]{0:T(128)S(1)} %pad_maximum_fusion.9, f32[]{:T(128)S(6)} %convert_element_type.207), channel_id=1, replica_groups=mesh['dp'=16,'mp'=2] {'dp'}, use_global_device_ids=true, to_apply=%region_23.24 | all-reduce | flops 4 | bytes 32 | tf_op jit(solution)/shard_map/psum | solution.py:170
  581.1 7.9 %multiply_reduce_fusion.2 = (f32[]{:T(128)}, f32[]{:T(128)}, f32[960,384]{1,0:T(8,128)}, f32[960,384]{1,0:T(8,128)}, f32[960,384]{1,0:T(8,128)}) fusion(f32[960,384]{1,0:T(8,128)} %param.28, f32[960,384]{1,0:T(8,128)} %param.29, f32[960,384]{1,0:T(8,128)} %param.30, f32[]{:T(128)S(6)} %div.121, f32[384,384]{1,0:T(8,128)} %bitcast.53, s32[384]{0:T(512)S(1)} %copy-done.77), kind=kOutput, calls=%fused_computation.65 | convolution fusion | flops 1705328640 | bytes 9438732 | tf_op jit(solution)/shard_map/pr,pc->rc/dot_general | solution.py:239
  590.2 1.5 multiply_reduce_fusion.15
  591.7 4.5 convert_reduce_fusion
  596.2 1.6 multiply_reduce_fusion.13
  599.9 52.9 %all-reduce.4 = (f32[4,768]{1,0:T(4,128)}, f32[8]{0:T(128)}, f32[8]{0:T(128)}) all-reduce(f32[4,768]{1,0:T(4,128)} %maximum_multiply_fusion, f32[8]{0:T(128)} %pad_maximum_fusion.11, f32[8]{0:T(128)S(1)} %pad_maximum_fusion.10), channel_id=1, replica_groups=mesh['dp'=16,'mp'=2] {'dp','mp'}, use_global_device_ids=true, to_apply=%region_40.41 | all-reduce | flops 3088 | bytes 24704 | tf_op jit(solution)/shard_map/psum | solution.py:272
  654.8 1.5 multiply_reduce_fusion.16
  660.8 1.9 multiply_subtract_fusion
  (263 shorter events, 47.1 us)
Async XLA Ops:
  7.2 20.1 %copy-start.25 = (f32[960,384]{1,0:T(8,128)S(1)}, f32[960,384]{1,0:T(8,128)}, u32[]{:S(2)}) copy-start(f32[960,384]{1,0:T(8,128)} %param.28) | copy-start | bytes 4423684
  7.2 70.2 %all-gather.3.cloned.1.call-start = ((), (), s32[]{:S(2)}) async-start(), calls=%async_computation.5 | async-start | bytes 2506752 | tf_op jit(solution)/shard_map/all_gather | solution.py:85
  10.1 31.8 %copy-start.62 = (s32[384]{0:T(512)}, s32[384]{0:T(512)S(1)}, u32[]{:S(2)}) copy-start(s32[384]{0:T(512)S(1)} %convert_element_type.170) | copy-start | bytes 4612
  11.7 15.5 %all-to-all-start = ((s32[16,24,1]{1,2,0:T(1,128)}), s32[16,24,1]{1,2,0:T(1,128)S(1)}, u32[]{:S(2)}, u32[]{:S(2)}) async-start(s32[16,24,1]{1,2,0:T(1,128)} %bitcast), calls=%async_computation | async-start | bytes 16384 | tf_op jit(solution)/shard_map/all_to_all | solution.py:100
  20.8 11.5 %copy-start.78 = (s32[384]{0:T(512)S(1)}, s32[384]{0:T(512)}, u32[]{:S(2)}) copy-start(s32[384]{0:T(512)} %param.20) | copy-start | bytes 4612
  27.3 15.0 %copy-start.76 = (s32[384]{0:T(512)}, s32[384]{0:T(512)S(1)}, u32[]{:S(2)}) copy-start(s32[384]{0:T(512)S(1)} %sub.124) | copy-start | bytes 4612
  28.7 13.3 %all-to-all-start.1 = ((bf16[16,24,384]{2,1,0:T(8,128)(2,1)}), bf16[16,24,384]{2,1,0:T(8,128)(2,1)S(1)}, u32[]{:S(2)}, u32[]{:S(2)}) async-start(bf16[16,24,384]{2,1,0:T(8,128)(2,1)} %bitcast.1), calls=%async_computation.1 | async-start | bytes 589824 | tf_op jit(solution)/shard_map/all_to_all | solution.py:106
  32.2 78.6 %all-reduce.11.cloned.1.call-start = ((), (), s32[]{:S(2)}) async-start(), calls=%async_computation.6 | async-start | bytes 2359296 | tf_op jit(solution)/shard_map/psum | solution.py:154
  32.3 49.2 %copy-start.72 = (pred[384]{0:T(512)(128)(4,1)}, pred[384]{0:T(512)(128)(4,1)S(1)}, u32[]{:S(2)}) copy-start(pred[384]{0:T(512)(128)(4,1)S(1)} %broadcast_compare_fusion.1) | copy-start | bytes 1156
  44.6 37.0 %copy-start.6 = (bf16[384,768]{1,0:T(8,128)(2,1)}, bf16[384,768]{1,0:T(8,128)(2,1)S(1)}, u32[]{:S(2)}) copy-start(bf16[384,768]{1,0:T(8,128)(2,1)S(1)} %all_gather.9) | copy-start | bytes 1769476
  92.0 125.0 %all-gather.5.cloned.1.call-start = ((), (), s32[]{:S(2)}) async-start(), calls=%async_computation.7 | async-start | bytes 7520256 | tf_op jit(solution)/shard_map/all_gather | solution.py:86
  94.1 152.8 %all-reduce.13.cloned.1.call-start = ((), (), s32[]{:S(2)}) async-start(), calls=%async_computation.8 | async-start | bytes 2359296 | tf_op jit(solution)/shard_map/psum | solution.py:161
  112.8 134.1 %copy-start.50 = (f32[384]{0:T(512)}, f32[384]{0:T(512)S(1)}, u32[]{:S(2)}) copy-start(f32[384]{0:T(512)S(1)} %broadcast_multiply_fusion.4) | copy-start | bytes 4612
  114.1 107.7 %copy-start.64 = (f32[384]{0:T(512)}, f32[384]{0:T(512)S(1)}, u32[]{:S(2)}) copy-start(f32[384]{0:T(512)S(1)} %multiply_reduce_fusion.11) | copy-start | bytes 4612
  114.1 132.9 %copy-start.56 = (f32[384]{0:T(512)}, f32[384]{0:T(512)S(1)}, u32[]{:S(2)}) copy-start(f32[384]{0:T(512)S(1)} %fusion.90) | copy-start | bytes 4612
  228.8 55.5 %all-reduce.15.cloned.1.call-start = ((), (), s32[]{:S(2)}) async-start(), calls=%async_computation.9 | async-start | bytes 2359296 | tf_op jit(solution)/shard_map/psum | solution.py:182
  231.2 18.2 %copy-start.55 = (f32[768]{0:T(1024)S(1)}, f32[768]{0:T(1024)}, u32[]{:S(2)}) copy-start(f32[768]{0:T(1024)} %get-tuple-element.83) | copy-start | bytes 9220
  249.2 4.9 slice-start
  252.4 7.6 %slice-start.2 = ((s8[7077888]{0:T(1024)(128)(4,1)}), s8[2883584]{0:T(1024)(128)(4,1)S(1)}, s32[]{:S(2)}) async-start(s8[7077888]{0:T(1024)(128)(4,1)} %bitcast.166), calls=%async_computation.13 | async-start | bytes 5767168
  254.0 4.6 copy-start.14
  254.1 4.6 copy-start.75
  254.1 6.0 slice-start.3
  263.1 57.0 %all-reduce.17.cloned.1.call-start = ((), (), s32[]{:S(2)}) async-start(), calls=%async_computation.10 | async-start | bytes 1179648 | tf_op jit(solution)/shard_map/psum | solution.py:229
  297.1 23.0 %copy-start.4 = (f32[384,768]{1,0:T(8,128)S(1)}, f32[384,768]{1,0:T(8,128)}, u32[]{:S(2)}) copy-start(f32[384,768]{1,0:T(8,128)} %copy-done.3) | copy-start | bytes 3538948
  297.1 23.0 %copy-start.61 = (f32[384]{0:T(512)S(1)}, f32[384]{0:T(512)}, u32[]{:S(2)}) copy-start(f32[384]{0:T(512)} %copy-done.60) | copy-start | bytes 4612
  297.1 23.0 %copy-start.74 = (pred[384]{0:T(512)(128)(4,1)S(1)}, pred[384]{0:T(512)(128)(4,1)}, u32[]{:S(2)}) copy-start(pred[384]{0:T(512)(128)(4,1)} %copy-done.72) | copy-start | bytes 1156
  299.9 22.6 %copy-start.63 = (s32[384]{0:T(512)S(1)}, s32[384]{0:T(512)}, u32[]{:S(2)}) copy-start(s32[384]{0:T(512)} %copy-done.62) | copy-start | bytes 4612
  322.5 8.6 %copy-start.8 = (bf16[384,768]{1,0:T(8,128)(2,1)S(1)}, bf16[384,768]{1,0:T(8,128)(2,1)}, u32[]{:S(2)}) copy-start(bf16[384,768]{1,0:T(8,128)(2,1)} %copy-done.6) | copy-start | bytes 1769476
  322.5 8.6 %copy-start.22 = (bf16[384,768]{1,0:T(8,128)(2,1)S(1)}, bf16[384,768]{1,0:T(8,128)(2,1)}, u32[]{:S(2)}) copy-start(bf16[384,768]{1,0:T(8,128)(2,1)} %param.17) | copy-start | bytes 1769476
  322.5 8.6 %copy-start.44 = (bf16[1,384,384]{2,1,0:T(8,128)(2,1)S(1)}, bf16[1,384,384]{2,1,0:T(8,128)(2,1)}, u32[]{:S(2)}) copy-start(bf16[1,384,384]{2,1,0:T(8,128)(2,1)} %copy.117) | copy-start | bytes 884740
  324.2 23.5 %all-to-all-start.4 = ((f32[16,24,384]{2,1,0:T(8,128)}), f32[16,24,384]{2,1,0:T(8,128)}, u32[]{:S(2)}, u32[]{:S(2)}) async-start(f32[16,24,384]{2,1,0:T(8,128)} %bitcast.52), calls=%async_computation.4 | async-start | bytes 1179648 | tf_op jit(solution)/shard_map/all_to_all | solution.py:238
  339.3 12.9 %copy-start.2 = (f32[384,768]{1,0:T(8,128)S(1)}, f32[384,768]{1,0:T(8,128)}, u32[]{:S(2)}) copy-start(f32[384,768]{1,0:T(8,128)} %copy-done) | copy-start | bytes 3538948
  339.3 12.9 %copy-start.52 = (f32[384]{0:T(512)S(1)}, f32[384]{0:T(512)}, u32[]{:S(2)}) copy-start(f32[384]{0:T(512)} %copy-done.50) | copy-start | bytes 4612
  339.3 12.9 %copy-start.58 = (f32[384]{0:T(512)S(1)}, f32[384]{0:T(512)}, u32[]{:S(2)}) copy-start(f32[384]{0:T(512)} %copy-done.56) | copy-start | bytes 4612
  339.3 12.9 %copy-start.69 = (f32[768]{0:T(1024)S(1)}, f32[768]{0:T(1024)}, u32[]{:S(2)}) copy-start(f32[768]{0:T(1024)} %get-tuple-element.85) | copy-start | bytes 9220
  347.7 51.4 %all-to-all-start.2 = ((bf16[16,4,48,384]{3,2,1,0:T(8,128)(2,1)}), bf16[16,4,48,384]{3,2,1,0:T(8,128)(2,1)S(1)}, u32[]{:S(2)}, u32[]{:S(2)}) async-start(bf16[16,4,48,384]{3,2,1,0:T(8,128)(2,1)} %copy.124), calls=%async_computation.2 | async-start | bytes 4718592 | tf_op jit(solution)/shard_map/all_to_all | solution.py:26
  368.6 210.0 %copy-start.71 = (f32[768]{0:T(1024)S(1)}, f32[768]{0:T(1024)}, u32[]{:S(2)}) copy-start(f32[768]{0:T(1024)} %get-tuple-element.73) | copy-start | bytes 9220
  368.6 211.3 %copy-start.70 = (f32[768]{0:T(1024)S(1)}, f32[768]{0:T(1024)}, u32[]{:S(2)}) copy-start(f32[768]{0:T(1024)} %get-tuple-element.80) | copy-start | bytes 9220
  368.6 211.9 %copy-start.68 = (f32[768]{0:T(1024)S(1)}, f32[768]{0:T(1024)}, u32[]{:S(2)}) copy-start(f32[768]{0:T(1024)} %get-tuple-element.71) | copy-start | bytes 9220
  368.6 211.9 %copy-start.67 = (f32[768]{0:T(1024)S(1)}, f32[768]{0:T(1024)}, u32[]{:S(2)}) copy-start(f32[768]{0:T(1024)} %get-tuple-element.77) | copy-start | bytes 9220
  368.6 212.5 %copy-start.77 = (s32[384]{0:T(512)S(1)}, s32[384]{0:T(512)}, u32[]{:S(2)}) copy-start(s32[384]{0:T(512)} %copy-done.76) | copy-start | bytes 4612
  399.1 192.6 %all-to-all-start.3 = ((bf16[16,3,48,1536]{3,2,1,0:T(8,128)(2,1)}), bf16[16,3,48,1536]{3,2,1,0:T(8,128)(2,1)}, u32[]{:S(2)}, u32[]{:S(2)}) async-start(bf16[16,3,48,1536]{3,2,1,0:T(8,128)(2,1)} %maximum_bitcast_fusion), calls=%async_computation.3 | async-start | bytes 14155776 | tf_op jit(solution)/shard_map/all_to_all | solution.py:26
  591.7 66.0 %copy-start.39 = (f32[4,48,384]{2,1,0:T(8,128)}, f32[4,48,384]{2,1,0:T(8,128)S(1)}, u32[]{:S(2)}) copy-start(f32[4,48,384]{2,1,0:T(8,128)S(1)} %get-tuple-element.100) | copy-start | bytes 884740
  591.7 66.0 %copy-start.40 = (f32[4,48,384]{2,1,0:T(8,128)}, f32[4,48,384]{2,1,0:T(8,128)S(1)}, u32[]{:S(2)}) copy-start(f32[4,48,384]{2,1,0:T(8,128)S(1)} %get-tuple-element.101) | copy-start | bytes 884740
  591.7 4.5 copy-start.41
  596.2 58.5 %copy-start.49 = (f32[4,768]{1,0:T(4,128)S(1)}, f32[4,768]{1,0:T(4,128)}, u32[]{:S(2)}) copy-start(f32[4,768]{1,0:T(4,128)} %param.31) | copy-start | bytes 36868
  597.9 62.1 %copy-start.16 = (f32[3,48,1536]{2,1,0:T(8,128)}, f32[3,48,1536]{2,1,0:T(8,128)S(1)}, u32[]{:S(2)}) copy-start(f32[3,48,1536]{2,1,0:T(8,128)S(1)} %get-tuple-element.103) | copy-start | bytes 2654212
  597.9 62.1 %copy-start.17 = (f32[3,48,1536]{2,1,0:T(8,128)}, f32[3,48,1536]{2,1,0:T(8,128)S(1)}, u32[]{:S(2)}) copy-start(f32[3,48,1536]{2,1,0:T(8,128)S(1)} %get-tuple-element.104) | copy-start | bytes 2654212
  (51 other events, 107.3 us)
Sparse Core Ops, SparseCore 0:
  11.4 65.9 all-gather.2
  92.2 18.6 all-reduce.10
  114.4 102.5 all-gather.4
  228.9 17.9 all-reduce.12
  263.2 20.9 all-reduce.14
  300.1 20.0 all-reduce.16
where the time goes:
time: 680 us; the launch traced here: 670 us
  waiting for transfers between devices  261 us (38%)
  blocking collectives  221 us (32%)
  matrix products  52.3 us (8%)
  other arithmetic  52.2 us (8%)
  starting transfers between devices  35 us (5%)
  local copies, waits for them, and re-layouts  30.1 us (4%)
  between operations  18.1 us (3%)
    psum x1, blocking collectives, local(): count_total, square_total = lax.psum((token_count, squares), 'dp')  166 us
    all_gather x1, waiting for transfers between devices, local(): lax.all_gather(geglu_master.astype(half_type), 'dp', axis=1, tiled=True)  103 us
    psum x1, blocking collectives, local(): lax.psum((weight_squares, update_squares, norms_local * 0.5), ('dp', 'mp'))  52.9 us
    all_gather x1, waiting for transfers between devices, local(): lax.all_gather(attention_master.astype(half_type), 'dp', axis=1, tiled=True)  32.8 us
    all_to_all x2, waiting for transfers between devices, sent_and_summed(): lax.all_to_all(cut_along(value, dim, length), axis, 0, 0, tiled=True)  30.5 us
    psum x1, waiting for transfers between devices, local(): grad_normed = grad_second + lax.psum(back_part, 'mp')  20.2 us
    psum x1, waiting for transfers between devices, local(): lax.psum(act_part.astype(jnp.bfloat16), 'mp').astype(jnp.float32)  20.2 us
    unnamed x178, local copies, waits for them, and re-layouts  19.1 us
  transfers between devices with their start and end apart: 11, of which 10 were waited for; matrix products, arithmetic and copies ran while one was open for 8% of the time, Pallas kernels for 0%

commit v1 on v0

--- a/solution.py
+++ b/solution.py
@@ -270,7 +270,7 @@
     )
     norms_local = jnp.concatenate([norm_grad_one, norm_grad_two], axis=0)
     weight_total, update_total, norms_summed = lax.psum(
-        (weight_squares, update_squares, norms_local * 0.5), ("dp", "mp")
+        lax.psum((weight_squares, update_squares, norms_local * 0.5), "mp"), "dp"
     )
     weight_norms = jnp.sqrt(weight_total)
     update_norms = jnp.sqrt(update_total)

time: 680 us -> 720 us (1.059)
  blocking collectives: 221 us -> 260 us
    psum x1 -> x2, blocking collectives: 166 us -> 253 us  [local(): count_total, square_total = lax.psum((token_count, squares), 'dp')]
    psum x1, blocking collectives: 52.9 us -> 4.57 us  [local(): lax.psum((weight_squares, update_squares, norms_local * 0.5), 'mp')]
  transfers between devices with their start and end apart: 11 -> 11, of which waited for: 10 -> 10; matrix products, arithmetic and copies ran while one was open for 8% -> 7% of each run, Pallas kernels for 0% -> 0%
where the time goes in v1:
time: 720 us; the launch traced here: 710 us
  waiting for transfers between devices  261 us (36%)
  blocking collectives  260 us (36%)
  other arithmetic  53.5 us (7%)
  matrix products  52.3 us (7%)
  starting transfers between devices  34.9 us (5%)
  local copies, waits for them, and re-layouts  30.1 us (4%)
  between operations  18.1 us (3%)
    psum x2, blocking collectives, local(): count_total, square_total = lax.psum((token_count, squares), 'dp')  253 us
    all_gather x1, waiting for transfers between devices, local(): lax.all_gather(geglu_master.astype(half_type), 'dp', axis=1, tiled=True)  103 us
    all_gather x1, waiting for transfers between devices, local(): lax.all_gather(attention_master.astype(half_type), 'dp', axis=1, tiled=True)  32.8 us
    all_to_all x2, waiting for transfers between devices, sent_and_summed(): lax.all_to_all(cut_along(value, dim, length), axis, 0, 0, tiled=True)  30.5 us
    psum x1, waiting for transfers between devices, local(): grad_normed = grad_second + lax.psum(back_part, 'mp')  20.2 us
    psum x1, waiting for transfers between devices, local(): lax.psum(act_part.astype(jnp.bfloat16), 'mp').astype(jnp.float32)  20.2 us
    unnamed x178, local copies, waits for them, and re-layouts  19.1 us
    psum x1, waiting for transfers between devices, local(): attn_out = lax.psum(attn_part, 'mp')  16 us
  transfers between devices with their start and end apart: 11, of which 10 were waited for; matrix products, arithmetic and copies ran while one was open for 7% of the time, Pallas kernels for 0%

profile of v1, /device:TPU:0, one launch (start us, length us, event | category | flops | bytes accessed | tf_op | source)
XLA Modules:
  0.0 709.8 jit_solution(3312694267128699533)
XLA Ops:
  7.2 1.8 copy.145
  11.7 8.3 %all-to-all-start = ((s32[16,24,1]{1,2,0:T(1,128)}), s32[16,24,1]{1,2,0:T(1,128)S(1)}, u32[]{:S(2)}, u32[]{:S(2)}) async-start(s32[16,24,1]{1,2,0:T(1,128)} %bitcast), calls=%async_computation | async-start | bytes 16384 | tf_op jit(solution)/shard_map/all_to_all | solution.py:100
  21.8 5.4 all-to-all-done
  28.7 3.5 all-to-all-start.1
  33.1 8.8 %all-to-all-done.1 = bf16[16,24,384]{2,1,0:T(8,128)(2,1)S(1)} async-done(((bf16[16,24,384]{2,1,0:T(8,128)(2,1)}), bf16[16,24,384]{2,1,0:T(8,128)(2,1)S(1)}, u32[]{:S(2)}, u32[]{:S(2)}) %all-to-all-start.1) | async-done | bytes 294944 | tf_op jit(solution)/shard_map/all_to_all | solution.py:106
  42.4 2.2 all_gather.9
  44.6 32.8 %all-gather.3.cloned.1.call-done = bf16[4,768,384]{2,0,1:T(4,128)(2,1)} async-done(((bf16[4,48,384]{2,0,1:T(4,128)(2,1)}), bf16[4,768,384]{2,0,1:T(4,128)(2,1)}) %all-gather.3.cloned.1.call-update) | async-done | bytes 2359312 | tf_op jit(solution)/shard_map/all_gather | solution.py:85
  77.4 4.1 copy.139
  90.4 1.5 fusion.79
  92.0 2.0 convert_element_type.187
  94.7 16.0 %all-reduce.11.cloned.1.call-done = f32[384,768]{1,0:T(8,128)} async-done(((f32[384,768]{1,0:T(8,128)}), f32[384,768]{1,0:T(8,128)}) %all-reduce.11.cloned.1.call-update) | async-done | bytes 1179664 | tf_op jit(solution)/shard_map/psum | solution.py:154
  110.8 2.0 fusion.110
  114.0 102.9 %all-gather.5.cloned.1.call-done = bf16[3,768,1536]{2,1,0:T(8,128)(2,1)} async-done(((bf16[3,48,1536]{2,1,0:T(8,128)(2,1)}), bf16[3,768,1536]{2,1,0:T(8,128)(2,1)}) %all-gather.5.cloned.1.call-update) | async-done | bytes 7077904 | tf_op jit(solution)/shard_map/all_gather | solution.py:86
  217.0 4.8 fusion.4
  224.9 3.8 fusion.31
  231.2 15.7 %all-reduce.13.cloned.1.call-done = f32[384,768]{1,0:T(8,128)} async-done(((f32[384,768]{1,0:T(8,128)}), f32[384,768]{1,0:T(8,128)}) %all-reduce.13.cloned.1.call-update) | async-done | bytes 1179664 | tf_op jit(solution)/shard_map/psum | solution.py:161
  246.9 2.2 fusion.108
  250.4 1.9 multiply_reduce_fusion.3
  252.3 1.7 fusion.107
  254.0 4.5 fusion.58
  260.0 3.0 fusion.40
  264.0 20.2 %all-reduce.15.cloned.1.call-done = f32[384,768]{1,0:T(8,128)} async-done(((f32[384,768]{1,0:T(8,128)}), f32[384,768]{1,0:T(8,128)}) %all-reduce.15.cloned.1.call-update) | async-done | bytes 1179664 | tf_op jit(solution)/shard_map/psum | solution.py:182
  284.2 4.1 multiply_reduce_fusion.4
  290.5 1.5 fusion.46
  297.0 2.8 fusion.44
  299.9 20.2 %all-reduce.17.cloned.1.call-done = bf16[384,768]{1,0:T(8,128)(2,1)} async-done(((bf16[384,768]{1,0:T(8,128)(2,1)}), bf16[384,768]{1,0:T(8,128)(2,1)}) %all-reduce.17.cloned.1.call-update) | async-done | bytes 589840 | tf_op jit(solution)/shard_map/psum | solution.py:229
  320.1 2.4 broadcast_select_fusion
  322.4 1.7 fusion.71
  324.1 6.8 all-to-all-start.4
  331.0 2.5 convert_bitcast_fusion
  333.5 2.8 copy.121
  337.4 1.8 copy.124
  339.3 8.4 %all-to-all-done.4 = f32[16,24,384]{2,1,0:T(8,128)} async-done(((f32[16,24,384]{2,1,0:T(8,128)}), f32[16,24,384]{2,1,0:T(8,128)}, u32[]{:S(2)}, u32[]{:S(2)}) %all-to-all-start.4) | async-done | bytes 589856 | tf_op jit(solution)/shard_map/all_to_all | solution.py:238
  347.7 4.5 all-to-all-start.2
  352.2 6.6 convolution_convert_fusion
  360.2 2.7 fusion.8
  362.8 5.7 maximum_bitcast_fusion
  368.5 30.5 %all-to-all-done.2 = bf16[16,4,48,384]{3,2,1,0:T(8,128)(2,1)S(1)} async-done(((bf16[16,4,48,384]{3,2,1,0:T(8,128)(2,1)}), bf16[16,4,48,384]{3,2,1,0:T(8,128)(2,1)S(1)}, u32[]{:S(2)}, u32[]{:S(2)}) %all-to-all-start.2) | async-done | bytes 2359328 | tf_op jit(solution)/shard_map/all_to_all | solution.py:26
  399.0 10.9 %all-to-all-start.3 = ((bf16[16,3,48,1536]{3,2,1,0:T(8,128)(2,1)}), bf16[16,3,48,1536]{3,2,1,0:T(8,128)(2,1)}, u32[]{:S(2)}, u32[]{:S(2)}) async-start(bf16[16,3,48,1536]{3,2,1,0:T(8,128)(2,1)} %maximum_bitcast_fusion), calls=%async_computation.3 | async-start | bytes 14155776 | tf_op jit(solution)/shard_map/all_to_all | solution.py:26
  410.6 167.9 %psum.89 = f32[]{:T(128)} all-reduce(f32[]{:T(128)S(6)} %convert_element_type.207), channel_id=1, replica_groups=mesh['dp'=16,'mp'=2] {'dp'}, use_global_device_ids=true, to_apply=%region_24.25 | all-reduce | flops 1 | bytes 8 | tf_op jit(solution)/shard_map/psum | solution.py:170
  579.9 2.0 pad_maximum_fusion.9
  582.6 7.9 %multiply_reduce_fusion.2 = (f32[]{:T(128)}, f32[]{:T(128)}, f32[960,384]{1,0:T(8,128)}, f32[960,384]{1,0:T(8,128)}, f32[960,384]{1,0:T(8,128)}) fusion(f32[960,384]{1,0:T(8,128)} %param.28, f32[960,384]{1,0:T(8,128)} %param.29, f32[960,384]{1,0:T(8,128)} %param.30, f32[]{:T(128)S(6)} %div.121, f32[384,384]{1,0:T(8,128)} %bitcast.53, s32[384]{0:T(512)S(1)} %copy-done.77), kind=kOutput, calls=%fused_computation.65 | convolution fusion | flops 1705328640 | bytes 9438732 | tf_op jit(solution)/shard_map/pr,pc->rc/dot_general | solution.py:239
  593.1 4.5 convert_reduce_fusion
  597.7 1.6 multiply_reduce_fusion.13
  601.8 4.6 all-reduce.5
  606.4 85.2 %all-reduce.4 = (f32[3]{0:T(128)}, f32[4,768]{1,0:T(4,128)}, f32[8]{0:T(128)}, f32[8]{0:T(128)}) all-reduce(f32[3]{0:T(128)S(1)} %pad_maximum_fusion.9, f32[4,768]{1,0:T(4,128)} %get-tuple-element.94, f32[8]{0:T(128)} %get-tuple-element.95, f32[8]{0:T(128)} %get-tuple-element.96), channel_id=1, replica_groups=mesh['dp'=16,'mp'=2] {'dp'}, use_global_device_ids=true, to_apply=%region_23.24 | all-reduce | flops 3091 | bytes 24728 | tf_op jit(solution)/shard_map/psum | solution.py:170
  694.8 1.5 multiply_reduce_fusion.16
  700.9 1.9 multiply_subtract_fusion
  (264 shorter events, 49.6 us)
Async XLA Ops:
  7.2 20.1 %copy-start.25 = (f32[960,384]{1,0:T(8,128)S(1)}, f32[960,384]{1,0:T(8,128)}, u32[]{:S(2)}) copy-start(f32[960,384]{1,0:T(8,128)} %param.28) | copy-start | bytes 4423684
  7.2 70.2 %all-gather.3.cloned.1.call-start = ((), (), s32[]{:S(2)}) async-start(), calls=%async_computation.5 | async-start | bytes 2506752 | tf_op jit(solution)/shard_map/all_gather | solution.py:85
  10.1 31.8 %copy-start.62 = (s32[384]{0:T(512)}, s32[384]{0:T(512)S(1)}, u32[]{:S(2)}) copy-start(s32[384]{0:T(512)S(1)} %convert_element_type.170) | copy-start | bytes 4612
  11.7 15.5 %all-to-all-start = ((s32[16,24,1]{1,2,0:T(1,128)}), s32[16,24,1]{1,2,0:T(1,128)S(1)}, u32[]{:S(2)}, u32[]{:S(2)}) async-start(s32[16,24,1]{1,2,0:T(1,128)} %bitcast), calls=%async_computation | async-start | bytes 16384 | tf_op jit(solution)/shard_map/all_to_all | solution.py:100
  20.8 11.5 %copy-start.78 = (s32[384]{0:T(512)S(1)}, s32[384]{0:T(512)}, u32[]{:S(2)}) copy-start(s32[384]{0:T(512)} %param.20) | copy-start | bytes 4612
  27.3 15.0 %copy-start.76 = (s32[384]{0:T(512)}, s32[384]{0:T(512)S(1)}, u32[]{:S(2)}) copy-start(s32[384]{0:T(512)S(1)} %sub.124) | copy-start | bytes 4612
  28.7 13.3 %all-to-all-start.1 = ((bf16[16,24,384]{2,1,0:T(8,128)(2,1)}), bf16[16,24,384]{2,1,0:T(8,128)(2,1)S(1)}, u32[]{:S(2)}, u32[]{:S(2)}) async-start(bf16[16,24,384]{2,1,0:T(8,128)(2,1)} %bitcast.1), calls=%async_computation.1 | async-start | bytes 589824 | tf_op jit(solution)/shard_map/all_to_all | solution.py:106
  32.2 78.5 %all-reduce.11.cloned.1.call-start = ((), (), s32[]{:S(2)}) async-start(), calls=%async_computation.6 | async-start | bytes 2359296 | tf_op jit(solution)/shard_map/psum | solution.py:154
  32.3 49.3 %copy-start.72 = (pred[384]{0:T(512)(128)(4,1)}, pred[384]{0:T(512)(128)(4,1)S(1)}, u32[]{:S(2)}) copy-start(pred[384]{0:T(512)(128)(4,1)S(1)} %broadcast_compare_fusion.1) | copy-start | bytes 1156
  44.6 37.0 %copy-start.6 = (bf16[384,768]{1,0:T(8,128)(2,1)}, bf16[384,768]{1,0:T(8,128)(2,1)S(1)}, u32[]{:S(2)}) copy-start(bf16[384,768]{1,0:T(8,128)(2,1)S(1)} %all_gather.9) | copy-start | bytes 1769476
  92.0 125.0 %all-gather.5.cloned.1.call-start = ((), (), s32[]{:S(2)}) async-start(), calls=%async_computation.7 | async-start | bytes 7520256 | tf_op jit(solution)/shard_map/all_gather | solution.py:86
  94.0 152.8 %all-reduce.13.cloned.1.call-start = ((), (), s32[]{:S(2)}) async-start(), calls=%async_computation.8 | async-start | bytes 2359296 | tf_op jit(solution)/shard_map/psum | solution.py:161
  112.8 134.1 %copy-start.50 = (f32[384]{0:T(512)}, f32[384]{0:T(512)S(1)}, u32[]{:S(2)}) copy-start(f32[384]{0:T(512)S(1)} %broadcast_multiply_fusion.4) | copy-start | bytes 4612
  114.0 107.7 %copy-start.64 = (f32[384]{0:T(512)}, f32[384]{0:T(512)S(1)}, u32[]{:S(2)}) copy-start(f32[384]{0:T(512)S(1)} %multiply_reduce_fusion.11) | copy-start | bytes 4612
  114.0 132.8 %copy-start.56 = (f32[384]{0:T(512)}, f32[384]{0:T(512)S(1)}, u32[]{:S(2)}) copy-start(f32[384]{0:T(512)S(1)} %fusion.90) | copy-start | bytes 4612
  228.8 55.4 %all-reduce.15.cloned.1.call-start = ((), (), s32[]{:S(2)}) async-start(), calls=%async_computation.9 | async-start | bytes 2359296 | tf_op jit(solution)/shard_map/psum | solution.py:182
  231.2 18.3 %copy-start.55 = (f32[768]{0:T(1024)S(1)}, f32[768]{0:T(1024)}, u32[]{:S(2)}) copy-start(f32[768]{0:T(1024)} %get-tuple-element.83) | copy-start | bytes 9220
  249.1 4.9 slice-start
  252.3 7.6 %slice-start.2 = ((s8[7077888]{0:T(1024)(128)(4,1)}), s8[2883584]{0:T(1024)(128)(4,1)S(1)}, s32[]{:S(2)}) async-start(s8[7077888]{0:T(1024)(128)(4,1)} %bitcast.166), calls=%async_computation.13 | async-start | bytes 5767168
  254.0 4.5 copy-start.14
  254.0 4.5 copy-start.75
  254.0 5.9 slice-start.3
  263.0 57.0 %all-reduce.17.cloned.1.call-start = ((), (), s32[]{:S(2)}) async-start(), calls=%async_computation.10 | async-start | bytes 1179648 | tf_op jit(solution)/shard_map/psum | solution.py:229
  297.0 23.0 %copy-start.4 = (f32[384,768]{1,0:T(8,128)S(1)}, f32[384,768]{1,0:T(8,128)}, u32[]{:S(2)}) copy-start(f32[384,768]{1,0:T(8,128)} %copy-done.3) | copy-start | bytes 3538948
  297.0 23.0 %copy-start.61 = (f32[384]{0:T(512)S(1)}, f32[384]{0:T(512)}, u32[]{:S(2)}) copy-start(f32[384]{0:T(512)} %copy-done.60) | copy-start | bytes 4612
  297.0 23.0 %copy-start.74 = (pred[384]{0:T(512)(128)(4,1)S(1)}, pred[384]{0:T(512)(128)(4,1)}, u32[]{:S(2)}) copy-start(pred[384]{0:T(512)(128)(4,1)} %copy-done.72) | copy-start | bytes 1156
  299.9 22.6 %copy-start.63 = (s32[384]{0:T(512)S(1)}, s32[384]{0:T(512)}, u32[]{:S(2)}) copy-start(s32[384]{0:T(512)} %copy-done.62) | copy-start | bytes 4612
  322.4 8.6 %copy-start.8 = (bf16[384,768]{1,0:T(8,128)(2,1)S(1)}, bf16[384,768]{1,0:T(8,128)(2,1)}, u32[]{:S(2)}) copy-start(bf16[384,768]{1,0:T(8,128)(2,1)} %copy-done.6) | copy-start | bytes 1769476
  322.4 8.6 %copy-start.22 = (bf16[384,768]{1,0:T(8,128)(2,1)S(1)}, bf16[384,768]{1,0:T(8,128)(2,1)}, u32[]{:S(2)}) copy-start(bf16[384,768]{1,0:T(8,128)(2,1)} %param.17) | copy-start | bytes 1769476
  322.4 8.6 %copy-start.44 = (bf16[1,384,384]{2,1,0:T(8,128)(2,1)S(1)}, bf16[1,384,384]{2,1,0:T(8,128)(2,1)}, u32[]{:S(2)}) copy-start(bf16[1,384,384]{2,1,0:T(8,128)(2,1)} %copy.117) | copy-start | bytes 884740
  324.1 23.5 %all-to-all-start.4 = ((f32[16,24,384]{2,1,0:T(8,128)}), f32[16,24,384]{2,1,0:T(8,128)}, u32[]{:S(2)}, u32[]{:S(2)}) async-start(f32[16,24,384]{2,1,0:T(8,128)} %bitcast.52), calls=%async_computation.4 | async-start | bytes 1179648 | tf_op jit(solution)/shard_map/all_to_all | solution.py:238
  339.3 12.9 %copy-start.2 = (f32[384,768]{1,0:T(8,128)S(1)}, f32[384,768]{1,0:T(8,128)}, u32[]{:S(2)}) copy-start(f32[384,768]{1,0:T(8,128)} %copy-done) | copy-start | bytes 3538948
  339.3 12.9 %copy-start.52 = (f32[384]{0:T(512)S(1)}, f32[384]{0:T(512)}, u32[]{:S(2)}) copy-start(f32[384]{0:T(512)} %copy-done.50) | copy-start | bytes 4612
  339.3 12.9 %copy-start.58 = (f32[384]{0:T(512)S(1)}, f32[384]{0:T(512)}, u32[]{:S(2)}) copy-start(f32[384]{0:T(512)} %copy-done.56) | copy-start | bytes 4612
  339.3 12.9 %copy-start.69 = (f32[768]{0:T(1024)S(1)}, f32[768]{0:T(1024)}, u32[]{:S(2)}) copy-start(f32[768]{0:T(1024)} %get-tuple-element.85) | copy-start | bytes 9220
  347.7 51.4 %all-to-all-start.2 = ((bf16[16,4,48,384]{3,2,1,0:T(8,128)(2,1)}), bf16[16,4,48,384]{3,2,1,0:T(8,128)(2,1)S(1)}, u32[]{:S(2)}, u32[]{:S(2)}) async-start(bf16[16,4,48,384]{3,2,1,0:T(8,128)(2,1)} %copy.124), calls=%async_computation.2 | async-start | bytes 4718592 | tf_op jit(solution)/shard_map/all_to_all | solution.py:26
  368.5 211.3 %copy-start.71 = (f32[768]{0:T(1024)S(1)}, f32[768]{0:T(1024)}, u32[]{:S(2)}) copy-start(f32[768]{0:T(1024)} %get-tuple-element.73) | copy-start | bytes 9220
  368.5 211.3 %copy-start.70 = (f32[768]{0:T(1024)S(1)}, f32[768]{0:T(1024)}, u32[]{:S(2)}) copy-start(f32[768]{0:T(1024)} %get-tuple-element.80) | copy-start | bytes 9220
  368.5 213.4 %copy-start.68 = (f32[768]{0:T(1024)S(1)}, f32[768]{0:T(1024)}, u32[]{:S(2)}) copy-start(f32[768]{0:T(1024)} %get-tuple-element.71) | copy-start | bytes 9220
  368.5 213.4 %copy-start.67 = (f32[768]{0:T(1024)S(1)}, f32[768]{0:T(1024)}, u32[]{:S(2)}) copy-start(f32[768]{0:T(1024)} %get-tuple-element.77) | copy-start | bytes 9220
  368.5 214.0 %copy-start.77 = (s32[384]{0:T(512)S(1)}, s32[384]{0:T(512)}, u32[]{:S(2)}) copy-start(s32[384]{0:T(512)} %copy-done.76) | copy-start | bytes 4612
  399.0 194.1 %all-to-all-start.3 = ((bf16[16,3,48,1536]{3,2,1,0:T(8,128)(2,1)}), bf16[16,3,48,1536]{3,2,1,0:T(8,128)(2,1)}, u32[]{:S(2)}, u32[]{:S(2)}) async-start(bf16[16,3,48,1536]{3,2,1,0:T(8,128)(2,1)} %maximum_bitcast_fusion), calls=%async_computation.3 | async-start | bytes 14155776 | tf_op jit(solution)/shard_map/all_to_all | solution.py:26
  593.1 104.6 %copy-start.39 = (f32[4,48,384]{2,1,0:T(8,128)}, f32[4,48,384]{2,1,0:T(8,128)S(1)}, u32[]{:S(2)}) copy-start(f32[4,48,384]{2,1,0:T(8,128)S(1)} %get-tuple-element.102) | copy-start | bytes 884740
  593.1 104.6 %copy-start.40 = (f32[4,48,384]{2,1,0:T(8,128)}, f32[4,48,384]{2,1,0:T(8,128)S(1)}, u32[]{:S(2)}) copy-start(f32[4,48,384]{2,1,0:T(8,128)S(1)} %get-tuple-element.103) | copy-start | bytes 884740
  593.1 4.5 copy-start.41
  597.7 97.1 %copy-start.49 = (f32[4,768]{1,0:T(4,128)S(1)}, f32[4,768]{1,0:T(4,128)}, u32[]{:S(2)}) copy-start(f32[4,768]{1,0:T(4,128)} %param.31) | copy-start | bytes 36868
  599.3 100.7 %copy-start.16 = (f32[3,48,1536]{2,1,0:T(8,128)}, f32[3,48,1536]{2,1,0:T(8,128)S(1)}, u32[]{:S(2)}) copy-start(f32[3,48,1536]{2,1,0:T(8,128)S(1)} %get-tuple-element.105) | copy-start | bytes 2654212
  599.3 100.7 %copy-start.17 = (f32[3,48,1536]{2,1,0:T(8,128)}, f32[3,48,1536]{2,1,0:T(8,128)S(1)}, u32[]{:S(2)}) copy-start(f32[3,48,1536]{2,1,0:T(8,128)S(1)} %get-tuple-element.106) | copy-start | bytes 2654212
  (51 other events, 107.6 us)
Sparse Core Ops, SparseCore 0:
  11.4 65.9 all-gather.2
  92.1 18.6 all-reduce.10
  114.4 102.5 all-gather.4
  228.9 17.9 all-reduce.12
  263.2 20.9 all-reduce.14
  300.0 20.0 all-reduce.16
